TPU v7x, 256 devices: a whole 4x4x8 slice. The times are simulated.
256 devices in a mesh: tx: 16 (over z, core), gx: 8 (over x, y_lo), gy: 2 (over y_hi).
Axes of the slice: x: 4, y: 4 (y_hi: 2, y_lo: 2; y = y_hi * 2 + y_lo), z: 8, core: 2. Of those that a mesh axis runs over, the one named last changes fastest.
Arguments:
- cond_h: float32 [128, 32, 128], P('gx', 'gy'), may hold values from 0.1 to 1.5
- cond_v: float32 [128, 32, 128], P('gx', 'gy'), may hold values from 0.1 to 1.5
- fwd_init: float32 [16, 6, 128, 32, 128], P('tx', None, 'gx', 'gy'), may hold values from -6 to 6
- adj_init: float32 [16, 6, 128, 32, 128], P('tx', None, 'gx', 'gy'), may hold values from -6 to 6
- observed: float32 [16, 4, 8, 2, 2, 32], P('tx', None, 'gx', 'gy'), may hold values from -6 to 6
- footprint: int32 [16, 8, 2], P('tx', 'gx', 'gy'), may hold values 0 or 1
- owner: int32 [8, 2, 16], P('gx', 'gy'), may hold values from 0 to 15, each once within a row
- rec_cells: int32 [8, 2, 32], P('gx', 'gy'), may hold values from 0 to 255
Outputs:
- owned_gradient: float32 [8, 16, 2, 1, 32, 128], P('gx', 'tx', None, None, 'gy')
- misfit: float32 [], replicated
Inputs may be any that keep to these rules, and one draw needn't show every extreme that they name: `owner`: each tile's row is a permutation of 0 to 15. `rec_cells`: cell index x * 16 + y within the tile; receivers may share a cell. `footprint`: 1 where the group's gradient counts in the tile.
All inputs are finite; a program needn't handle non-finite values.
Results may differ from a plain program's by a relative error of at most 0.00028.
Values sent between devices are 32-bit elements; how exact they have to be, the bound alone decides.
No kernel may reach another device: no remote copies, remote signals or barrier semaphores. Data moves between devices by JAX's collectives and lax.ppermute only.
A program may use at most 64 MiB of HBM per device.

v0:
```python
import jax
import jax.numpy as jnp
from jax import lax
from jax.sharding import PartitionSpec as P

STEPS = 4
ZREC = 32
STEP_DT = 0.5


def shifted(x, axis, by):
    size = lax.axis_size(axis)
    pairs = [(i, i + by) for i in range(size) if 0 <= i + by < size]
    return lax.ppermute(x, axis, pairs)


def coefficients(conduct):
    half_rate = 0.25 * conduct
    return ((1.0 - half_rate) / (1.0 + half_rate), STEP_DT / (1.0 + half_rate))


def ahead_of(values, tail_plane, axis_num):
    extent = values.shape[axis_num]
    return jnp.concatenate(
        [lax.slice_in_dim(values, 1, extent, axis=axis_num), tail_plane], axis=axis_num
    )


def before(values, head_plane, axis_num):
    extent = values.shape[axis_num]
    return jnp.concatenate(
        [head_plane, lax.slice_in_dim(values, 0, extent - 1, axis=axis_num)], axis=axis_num
    )


def zero_plane(values, axis_num):
    return jnp.zeros_like(lax.slice_in_dim(values, 0, 1, axis=axis_num))


def curl_ahead(field, next_x, next_y):
    comp_x, comp_y, comp_z = (field[0], field[1], field[2])
    out_x = (
        ahead_of(comp_z, next_y[1], 1)
        - comp_z
        - (ahead_of(comp_y, zero_plane(comp_y, 2), 2) - comp_y)
    )
    out_y = (
        ahead_of(comp_x, zero_plane(comp_x, 2), 2)
        - comp_x
        - (ahead_of(comp_z, next_x[1], 0) - comp_z)
    )
    out_z = ahead_of(comp_y, next_x[0], 0) - comp_y - (ahead_of(comp_x, next_y[0], 1) - comp_x)
    return jnp.stack([out_x, out_y, out_z])


def curl_before(field, prev_x, prev_y):
    comp_x, comp_y, comp_z = (field[0], field[1], field[2])
    out_x = (
        comp_z - before(comp_z, prev_y[1], 1) - (comp_y - before(comp_y, zero_plane(comp_y, 2), 2))
    )
    out_y = (
        comp_x - before(comp_x, zero_plane(comp_x, 2), 2) - (comp_z - before(comp_z, prev_x[1], 0))
    )
    out_z = comp_y - before(comp_y, prev_x[0], 0) - (comp_x - before(comp_x, prev_y[0], 1))
    return jnp.stack([out_x, out_y, out_z])


def electric_rims(electric):
    next_x = shifted(electric[1:3, 0:1], "gx", -1)
    next_y = shifted(electric[0::2, :, 0:1], "gy", -1)
    return (next_x, next_y)


def magnetic_rims(magnetic):
    size_x = magnetic.shape[1]
    size_y = magnetic.shape[2]
    prev_x = shifted(magnetic[1:3, size_x - 1 : size_x], "gx", 1)
    prev_y = shifted(magnetic[0::2, :, size_y - 1 : size_y], "gy", 1)
    return (prev_x, prev_y)


def advance(electric, magnetic, decay, drive):
    next_x, next_y = electric_rims(electric)
    magnetic = magnetic - STEP_DT * curl_ahead(electric, next_x, next_y)
    prev_x, prev_y = magnetic_rims(magnetic)
    electric = decay * electric + drive * curl_before(magnetic, prev_x, prev_y)
    return (electric, magnetic)


def on_device(cond_h, cond_v, fwd_init, adj_init, observed, footprint, owner, rec_cells):
    size_x, size_y, depth = cond_h.shape
    decay_h, drive_h = coefficients(cond_h)
    decay_v, drive_v = coefficients(cond_v)
    highest = lax.Precision.HIGHEST
    cell_ids = jnp.arange(size_x * size_y, dtype=jnp.int32)
    onehot = (rec_cells[0, 0][:, None] == cell_ids[None, :]).astype(jnp.float32)
    observe = observed[0, :, 0, 0]
    grad_h = jnp.zeros((size_x, size_y, depth), jnp.float32)
    grad_v = jnp.zeros((size_x, size_y, depth), jnp.float32)
    residuals = []
    decay = jnp.stack([decay_h, decay_h, decay_v])
    drive = jnp.stack([drive_h, drive_h, drive_v])
    electric, magnetic = (fwd_init[0, 0:3], fwd_init[0, 3:6])
    stored = []
    for step_idx in range(STEPS):
        electric, magnetic = advance(electric, magnetic, decay, drive)
        stored.append(electric)
        planes = electric[0:2, :, :, ZREC].reshape(2, size_x * size_y)
        residuals.append(jnp.dot(planes, onehot.T, precision=highest) - observe[step_idx])
    adj_e, adj_h = (adj_init[0, 0:3], adj_init[0, 3:6])
    for step_idx in reversed(range(STEPS)):
        adj_e = adj_e.at[0:2, :, :, ZREC].add(
            jnp.dot(residuals[step_idx], onehot, precision=highest).reshape(2, size_x, size_y)
        )
        adj_e, adj_h = advance(adj_e, adj_h, decay, drive)
        kept = stored[step_idx]
        grad_h = grad_h + adj_e[0] * kept[0] + adj_e[1] * kept[1]
        grad_v = grad_v + adj_e[2] * kept[2]
    local_misfit = jnp.float32(0.0)
    for step_idx in range(STEPS):
        local_misfit = local_misfit + 0.5 * jnp.sum(residuals[step_idx] * residuals[step_idx])
    misfit = lax.psum(local_misfit, ("tx", "gx", "gy"))
    tile_flag = footprint[0, 0, 0].astype(jnp.float32)
    gradient = jnp.stack([grad_h, grad_v]) * tile_flag
    groups_count = lax.axis_size("tx")
    block_rows = size_x // groups_count
    blocked = gradient.reshape(2, groups_count, block_rows, size_y, depth)
    ordered = jnp.take(blocked, owner[0, 0], axis=1)
    summed = lax.psum_scatter(ordered, "tx", scatter_dimension=1, tiled=True)
    owned_part = summed.reshape(1, 1, 2, block_rows, size_y, depth)
    return (owned_part, misfit)


def solution(mesh):
    placed = (
        P("gx", "gy", None),
        P("gx", "gy", None),
        P("tx", None, "gx", "gy", None),
        P("tx", None, "gx", "gy", None),
        P("tx", None, "gx", "gy", None, None),
        P("tx", "gx", "gy"),
        P("gx", "gy", None),
        P("gx", "gy", None),
    )
    return jax.shard_map(
        on_device,
        mesh=mesh,
        in_specs=placed,
        out_specs=(P("gx", "tx", None, None, "gy", None), P()),
        check_vma=False,
    )
```

profile of v0, /device:TPU:1, one launch (start us, length us, event | category | flops | bytes accessed | tf_op | source)
XLA Modules:
  0.0 326.6 jit_solution(11279298193173657843)
XLA Ops:
  7.2 1.1 slice_bitcast_fusion
  8.3 1.3 collective-permute-start
  9.6 1.4 collective-permute-start.1
  12.4 0.9 copy-done.70
  15.4 2.0 and_reduce_fusion
  19.2 5.6 %collective-permute-start.2 = (f32[2,16,1,128]{3,1,2,0:T(8,128)S(1)}, f32[2,16,1,128]{3,1,2,0:T(8,128)S(1)}, u32[]{:S(2)}, u32[]{:S(2)}) collective-permute-start(f32[2,16,1,128]{3,1,2,0:T(8,128)S(1)} %bitcast.592), channel_id=1, source_target_pairs={{0,1},{2,3},{4,5},{6,7},{8,9},{10,11},{12,13},{14,15},{16,17},{18,... | collective-permute-start | bytes 49160 | tf_op jit(solution)/shard_map/ppermute | solution.py:14
  24.9 4.5 %collective-permute-start.3 = (f32[2,1,16,128]{3,2,1,0:T(8,128)S(1)}, f32[2,1,16,128]{3,2,1,0:T(8,128)S(1)}, u32[]{:S(2)}, u32[]{:S(2)}) collective-permute-start(f32[2,1,16,128]{3,2,1,0:T(8,128)S(1)} %slice.1340), channel_id=1, source_target_pairs={{0,2},{2,4},{4,6},{6,8},{8,10},{10,12},{12,14},{1,3},{3,5},{5,7},{... | collective-permute-start | bytes 49160 | tf_op jit(solution)/shard_map/ppermute | solution.py:14
  32.5 1.3 collective-permute-start.4
  33.8 1.3 collective-permute-start.5
  35.8 1.5 multiply_reduce_fusion.3
  37.5 0.9 reshape.515
  38.5 1.3 collective-permute-done.5
  41.6 6.1 %collective-permute-start.6 = (f32[2,16,1,128]{3,1,2,0:T(8,128)S(1)}, f32[2,16,1,128]{3,1,2,0:T(8,128)S(1)}, u32[]{:S(2)}, u32[]{:S(2)}) collective-permute-start(f32[2,16,1,128]{3,1,2,0:T(8,128)S(1)} %bitcast.593), channel_id=1, source_target_pairs={{0,1},{2,3},{4,5},{6,7},{8,9},{10,11},{12,13},{14,15},{16,17},{18,... | collective-permute-start | bytes 49160 | tf_op jit(solution)/shard_map/ppermute | solution.py:14
  47.8 3.7 %collective-permute-start.7 = (f32[2,1,16,128]{3,2,1,0:T(8,128)S(1)}, f32[2,1,16,128]{3,2,1,0:T(8,128)S(1)}, u32[]{:S(2)}, u32[]{:S(2)}) collective-permute-start(f32[2,1,16,128]{3,2,1,0:T(8,128)S(1)} %slice.1368), channel_id=1, source_target_pairs={{0,2},{2,4},{4,6},{6,8},{8,10},{10,12},{12,14},{1,3},{3,5},{5,7},{... | collective-permute-start | bytes 49160 | tf_op jit(solution)/shard_map/ppermute | solution.py:14
  56.2 1.6 multiply_reduce_fusion.2
  57.8 1.3 collective-permute-start.8
  59.1 1.3 collective-permute-start.9
  60.6 0.9 reshape.514
  61.5 2.3 collective-permute-done.8
  63.7 1.3 collective-permute-done.9
  65.0 0.9 slice_bitcast_fusion.79
  68.3 6.1 %collective-permute-start.10 = (f32[2,16,1,128]{3,1,2,0:T(8,128)S(1)}, f32[2,16,1,128]{3,1,2,0:T(8,128)S(1)}, u32[]{:S(2)}, u32[]{:S(2)}) collective-permute-start(f32[2,16,1,128]{3,1,2,0:T(8,128)S(1)} %bitcast.594), channel_id=1, source_target_pairs={{0,1},{2,3},{4,5},{6,7},{8,9},{10,11},{12,13},{14,15},{16,17},{18,... | collective-permute-start | bytes 49160 | tf_op jit(solution)/shard_map/ppermute | solution.py:14
  74.5 3.7 %collective-permute-start.11 = (f32[2,1,16,128]{3,2,1,0:T(8,128)S(1)}, f32[2,1,16,128]{3,2,1,0:T(8,128)S(1)}, u32[]{:S(2)}, u32[]{:S(2)}) collective-permute-start(f32[2,1,16,128]{3,2,1,0:T(8,128)S(1)} %slice.1396), channel_id=1, source_target_pairs={{0,2},{2,4},{4,6},{6,8},{8,10},{10,12},{12,14},{1,3},{3,5},{5,7},{... | collective-permute-start | bytes 49160 | tf_op jit(solution)/shard_map/ppermute | solution.py:14
  84.6 1.5 multiply_reduce_fusion.1
  86.1 1.4 collective-permute-start.12
  87.5 1.3 collective-permute-start.13
  89.6 1.6 reshape.513
  91.2 1.3 collective-permute-done.12
  94.0 1.0 slice_bitcast_fusion.77
  97.4 5.9 %collective-permute-start.14 = (f32[2,16,1,128]{3,1,2,0:T(8,128)S(1)}, f32[2,16,1,128]{3,1,2,0:T(8,128)S(1)}, u32[]{:S(2)}, u32[]{:S(2)}) collective-permute-start(f32[2,16,1,128]{3,1,2,0:T(8,128)S(1)} %bitcast.595), channel_id=1, source_target_pairs={{0,1},{2,3},{4,5},{6,7},{8,9},{10,11},{12,13},{14,15},{16,17},{18,... | collective-permute-start | bytes 49160 | tf_op jit(solution)/shard_map/ppermute | solution.py:14
  103.3 3.7 %collective-permute-start.15 = (f32[2,1,16,128]{3,2,1,0:T(8,128)S(1)}, f32[2,1,16,128]{3,2,1,0:T(8,128)S(1)}, u32[]{:S(2)}, u32[]{:S(2)}) collective-permute-start(f32[2,1,16,128]{3,2,1,0:T(8,128)S(1)} %slice.1424), channel_id=1, source_target_pairs={{0,2},{2,4},{4,6},{6,8},{8,10},{10,12},{12,14},{1,3},{3,5},{5,7},{... | collective-permute-start | bytes 49160 | tf_op jit(solution)/shard_map/ppermute | solution.py:14
  110.4 1.5 multiply_reduce_fusion
  112.3 2.0 add_select_fusion.3
  114.3 3.6 %scatter-add.14 = f32[3,16,16,128]{3,2,1,0:T(8,128)S(1)} dynamic-update-slice(f32[3,16,16,128]{3,2,1,0:T(8,128)S(1)} %get-tuple-element.51, f32[2,16,16,1]{3,2,1,0:T(8,128)S(1)} %add_select_fusion.3, s32[]{:T(128)} %bitcast.4, s32[]{:T(128)} %constant.106.clone.1, s32[]{:T(128)} %constant.106.clone.1, s32[]{:T(128)} %bitcast.5) | dynamic-update-slice | bytes 4100 | tf_op jit(solution)/shard_map/scatter-add | solution.py:112
  118.0 1.3 collective-permute-start.16
  119.4 1.3 collective-permute-start.17
  120.7 3.3 collective-permute-done.16
  124.0 0.9 collective-permute-done.17
  126.3 6.1 %collective-permute-start.18 = (f32[2,16,1,128]{3,1,2,0:T(8,128)S(1)}, f32[2,16,1,128]{3,1,2,0:T(8,128)S(1)}, u32[]{:S(2)}, u32[]{:S(2)}) collective-permute-start(f32[2,16,1,128]{3,1,2,0:T(8,128)S(1)} %bitcast.596), channel_id=1, source_target_pairs={{0,1},{2,3},{4,5},{6,7},{8,9},{10,11},{12,13},{14,15},{16,17},{18,... | collective-permute-start | bytes 49160 | tf_op jit(solution)/shard_map/ppermute | solution.py:14
  132.4 3.7 %collective-permute-start.19 = (f32[2,1,16,128]{3,2,1,0:T(8,128)S(1)}, f32[2,1,16,128]{3,2,1,0:T(8,128)S(1)}, u32[]{:S(2)}, u32[]{:S(2)}) collective-permute-start(f32[2,1,16,128]{3,2,1,0:T(8,128)S(1)} %slice.1453), channel_id=1, source_target_pairs={{0,2},{2,4},{4,6},{6,8},{8,10},{10,12},{12,14},{1,3},{3,5},{5,7},{... | collective-permute-start | bytes 49160 | tf_op jit(solution)/shard_map/ppermute | solution.py:14
  137.3 0.9 copy-done.65
  138.2 2.0 add_select_fusion.2
  140.3 3.6 %scatter-add.15 = f32[3,16,16,128]{3,2,1,0:T(8,128)S(1)} dynamic-update-slice(f32[3,16,16,128]{3,2,1,0:T(8,128)S(1)} %copy.87, f32[2,16,16,1]{3,2,1,0:T(8,128)S(1)} %add_select_fusion.2, s32[]{:T(128)} %bitcast.4, s32[]{:T(128)} %constant.106.clone.1, s32[]{:T(128)} %constant.106.clone.1, s32[]{:T(128)} %bitcast.5) | dynamic-update-slice | bytes 4100 | tf_op jit(solution)/shard_map/scatter-add | solution.py:112
  143.9 1.3 collective-permute-start.20
  145.4 1.3 collective-permute-start.21
  146.7 3.3 collective-permute-done.20
  151.7 6.1 %collective-permute-start.22 = (f32[2,16,1,128]{3,1,2,0:T(8,128)S(1)}, f32[2,16,1,128]{3,1,2,0:T(8,128)S(1)}, u32[]{:S(2)}, u32[]{:S(2)}) collective-permute-start(f32[2,16,1,128]{3,1,2,0:T(8,128)S(1)} %bitcast.597), channel_id=1, source_target_pairs={{0,1},{2,3},{4,5},{6,7},{8,9},{10,11},{12,13},{14,15},{16,17},{18,... | collective-permute-start | bytes 49160 | tf_op jit(solution)/shard_map/ppermute | solution.py:14
  157.8 3.7 %collective-permute-start.23 = (f32[2,1,16,128]{3,2,1,0:T(8,128)S(1)}, f32[2,1,16,128]{3,2,1,0:T(8,128)S(1)}, u32[]{:S(2)}, u32[]{:S(2)}) collective-permute-start(f32[2,1,16,128]{3,2,1,0:T(8,128)S(1)} %slice.1486), channel_id=1, source_target_pairs={{0,2},{2,4},{4,6},{6,8},{8,10},{10,12},{12,14},{1,3},{3,5},{5,7},{... | collective-permute-start | bytes 49160 | tf_op jit(solution)/shard_map/ppermute | solution.py:14
  162.7 0.9 copy-done.64
  163.6 2.0 add_select_fusion.1
  165.6 3.6 %scatter-add.16 = f32[3,16,16,128]{3,2,1,0:T(8,128)S(1)} dynamic-update-slice(f32[3,16,16,128]{3,2,1,0:T(8,128)S(1)} %copy.88, f32[2,16,16,1]{3,2,1,0:T(8,128)S(1)} %add_select_fusion.1, s32[]{:T(128)} %bitcast.4, s32[]{:T(128)} %constant.106.clone.1, s32[]{:T(128)} %constant.106.clone.1, s32[]{:T(128)} %bitcast.5) | dynamic-update-slice | bytes 4100 | tf_op jit(solution)/shard_map/scatter-add | solution.py:112
  169.3 1.3 collective-permute-start.24
  170.7 1.5 collective-permute-start.25
  172.2 3.1 collective-permute-done.24
  177.5 6.1 %collective-permute-start.26 = (f32[2,16,1,128]{3,1,2,0:T(8,128)S(1)}, f32[2,16,1,128]{3,1,2,0:T(8,128)S(1)}, u32[]{:S(2)}, u32[]{:S(2)}) collective-permute-start(f32[2,16,1,128]{3,1,2,0:T(8,128)S(1)} %bitcast.598), channel_id=1, source_target_pairs={{0,1},{2,3},{4,5},{6,7},{8,9},{10,11},{12,13},{14,15},{16,17},{18,... | collective-permute-start | bytes 49160 | tf_op jit(solution)/shard_map/ppermute | solution.py:14
  183.6 3.7 %collective-permute-start.27 = (f32[2,1,16,128]{3,2,1,0:T(8,128)S(1)}, f32[2,1,16,128]{3,2,1,0:T(8,128)S(1)}, u32[]{:S(2)}, u32[]{:S(2)}) collective-permute-start(f32[2,1,16,128]{3,2,1,0:T(8,128)S(1)} %slice.1517), channel_id=1, source_target_pairs={{0,2},{2,4},{4,6},{6,8},{8,10},{10,12},{12,14},{1,3},{3,5},{5,7},{... | collective-permute-start | bytes 49160 | tf_op jit(solution)/shard_map/ppermute | solution.py:14
  189.6 2.0 add_select_fusion
  191.6 3.6 %scatter-add.19 = f32[3,16,16,128]{3,2,1,0:T(8,128)S(1)} dynamic-update-slice(f32[3,16,16,128]{3,2,1,0:T(8,128)S(1)} %copy.89, f32[2,16,16,1]{3,2,1,0:T(8,128)S(1)} %add_select_fusion, s32[]{:T(128)} %bitcast.4, s32[]{:T(128)} %constant.106.clone.1, s32[]{:T(128)} %constant.106.clone.1, s32[]{:T(128)} %bitcast.5) | dynamic-update-slice | bytes 4100 | tf_op jit(solution)/shard_map/scatter-add | solution.py:112
  195.3 1.3 collective-permute-start.28
  196.7 1.3 collective-permute-start.29
  198.0 3.3 collective-permute-done.28
  203.1 6.1 %collective-permute-start.30 = (f32[2,16,1,128]{3,1,2,0:T(8,128)S(1)}, f32[2,16,1,128]{3,1,2,0:T(8,128)S(1)}, u32[]{:S(2)}, u32[]{:S(2)}) collective-permute-start(f32[2,16,1,128]{3,1,2,0:T(8,128)S(1)} %bitcast.599), channel_id=1, source_target_pairs={{0,1},{2,3},{4,5},{6,7},{8,9},{10,11},{12,13},{14,15},{16,17},{18,... | collective-permute-start | bytes 49160 | tf_op jit(solution)/shard_map/ppermute | solution.py:14
  209.3 3.7 %collective-permute-start.31 = (f32[2,1,16,128]{3,2,1,0:T(8,128)S(1)}, f32[2,1,16,128]{3,2,1,0:T(8,128)S(1)}, u32[]{:S(2)}, u32[]{:S(2)}) collective-permute-start(f32[2,1,16,128]{3,2,1,0:T(8,128)S(1)} %slice.1548), channel_id=1, source_target_pairs={{0,2},{2,4},{4,6},{6,8},{8,10},{10,12},{12,14},{1,3},{3,5},{5,7},{... | collective-permute-start | bytes 49160 | tf_op jit(solution)/shard_map/ppermute | solution.py:14
  219.5 100.3 %psum.7 = f32[]{:T(128)} all-reduce(f32[]{:T(128)S(6)} %add.229), channel_id=1, replica_groups=mesh['tx'=16,'gx'=8,'gy'=2] {'tx','gx','gy'}, use_global_device_ids=true, to_apply=%region_6.0 | all-reduce | flops 1 | bytes 8 | tf_op jit(solution)/shard_map/psum | solution.py:122
  (397 shorter events, 48.0 us)
Async XLA Ops:
  7.2 3.9 %copy-start = (f32[1,6,16,16,128]{4,3,2,1,0:T(8,128)S(1)}, f32[1,6,16,16,128]{4,3,2,1,0:T(8,128)}, u32[]{:S(2)}) copy-start(f32[1,6,16,16,128]{4,3,2,1,0:T(8,128)} %param.18) | copy-start | bytes 2359300
  7.2 312.6 %reduce-scatter.2.cloned.1.call-start = ((), (), s32[]{:S(2)}) async-start(), calls=%async_computation.1 | async-start | bytes 278528 | tf_op jit(solution)/shard_map/reduce_scatter | solution.py:129
  8.3 10.5 %collective-permute-start = (f32[2,16,1,128]{3,2,1,0:T(1,128)S(1)}, f32[2,16,1,128]{3,2,1,0:T(1,128)S(1)}, u32[]{:S(2)}, u32[]{:S(2)}) collective-permute-start(f32[2,16,1,128]{3,2,1,0:T(1,128)S(1)} %slice.1044), channel_id=1, source_target_pairs={{1,0},{3,2},{5,4},{7,6},{9,8},{11,10},{13,12},{15,14},{17,16},{19,... | collective-permute-start | bytes 49160 | tf_op jit(solution)/shard_map/ppermute | solution.py:14
  9.6 4.3 %copy-start.3 = (f32[1,6,16,16,128]{4,3,2,1,0:T(8,128)S(1)}, f32[1,6,16,16,128]{4,3,2,1,0:T(8,128)}, u32[]{:S(2)}) copy-start(f32[1,6,16,16,128]{4,3,2,1,0:T(8,128)} %param.19) | copy-start | bytes 2359300
  9.6 9.2 %collective-permute-start.1 = (f32[2,1,16,128]{3,2,1,0:T(8,128)S(1)}, f32[2,1,16,128]{3,2,1,0:T(8,128)S(1)}, u32[]{:S(2)}, u32[]{:S(2)}) collective-permute-start(f32[2,1,16,128]{3,2,1,0:T(8,128)S(1)} %slice.1328), channel_id=1, source_target_pairs={{2,0},{4,2},{6,4},{8,6},{10,8},{12,10},{14,12},{3,1},{5,3},{7,5},{... | collective-permute-start | bytes 49160 | tf_op jit(solution)/shard_map/ppermute | solution.py:14
  18.9 21.9 %copy-start.8 = (f32[1,16,16,128]{3,2,1,0:T(8,128)}, f32[1,16,16,128]{3,2,1,0:T(8,128)S(1)}, u32[]{:S(2)}) copy-start(f32[1,16,16,128]{3,2,1,0:T(8,128)S(1)} %fusion.33) | copy-start | bytes 393220
  19.2 10.2 %collective-permute-start.2 = (f32[2,16,1,128]{3,1,2,0:T(8,128)S(1)}, f32[2,16,1,128]{3,1,2,0:T(8,128)S(1)}, u32[]{:S(2)}, u32[]{:S(2)}) collective-permute-start(f32[2,16,1,128]{3,1,2,0:T(8,128)S(1)} %bitcast.592), channel_id=1, source_target_pairs={{0,1},{2,3},{4,5},{6,7},{8,9},{10,11},{12,13},{14,15},{16,17},{18,... | collective-permute-start | bytes 49160 | tf_op jit(solution)/shard_map/ppermute | solution.py:14
  24.9 5.4 %collective-permute-start.3 = (f32[2,1,16,128]{3,2,1,0:T(8,128)S(1)}, f32[2,1,16,128]{3,2,1,0:T(8,128)S(1)}, u32[]{:S(2)}, u32[]{:S(2)}) collective-permute-start(f32[2,1,16,128]{3,2,1,0:T(8,128)S(1)} %slice.1340), channel_id=1, source_target_pairs={{0,2},{2,4},{4,6},{6,8},{8,10},{10,12},{12,14},{1,3},{3,5},{5,7},{... | collective-permute-start | bytes 49160 | tf_op jit(solution)/shard_map/ppermute | solution.py:14
  32.5 6.0 %collective-permute-start.4 = (f32[2,16,1,128]{3,2,1,0:T(1,128)S(1)}, f32[2,16,1,128]{3,2,1,0:T(1,128)S(1)}, u32[]{:S(2)}, u32[]{:S(2)}) collective-permute-start(f32[2,16,1,128]{3,2,1,0:T(1,128)S(1)} %slice.1076), channel_id=1, source_target_pairs={{1,0},{3,2},{5,4},{7,6},{9,8},{11,10},{13,12},{15,14},{17,16},{19,... | collective-permute-start | bytes 49160 | tf_op jit(solution)/shard_map/ppermute | solution.py:14
  33.8 6.0 %collective-permute-start.5 = (f32[2,1,16,128]{3,2,1,0:T(8,128)S(1)}, f32[2,1,16,128]{3,2,1,0:T(8,128)S(1)}, u32[]{:S(2)}, u32[]{:S(2)}) collective-permute-start(f32[2,1,16,128]{3,2,1,0:T(8,128)S(1)} %slice.1355), channel_id=1, source_target_pairs={{2,0},{4,2},{6,4},{8,6},{10,8},{12,10},{14,12},{3,1},{5,3},{7,5},{... | collective-permute-start | bytes 49160 | tf_op jit(solution)/shard_map/ppermute | solution.py:14
  41.6 9.8 %collective-permute-start.6 = (f32[2,16,1,128]{3,1,2,0:T(8,128)S(1)}, f32[2,16,1,128]{3,1,2,0:T(8,128)S(1)}, u32[]{:S(2)}, u32[]{:S(2)}) collective-permute-start(f32[2,16,1,128]{3,1,2,0:T(8,128)S(1)} %bitcast.593), channel_id=1, source_target_pairs={{0,1},{2,3},{4,5},{6,7},{8,9},{10,11},{12,13},{14,15},{16,17},{18,... | collective-permute-start | bytes 49160 | tf_op jit(solution)/shard_map/ppermute | solution.py:14
  47.8 4.5 %collective-permute-start.7 = (f32[2,1,16,128]{3,2,1,0:T(8,128)S(1)}, f32[2,1,16,128]{3,2,1,0:T(8,128)S(1)}, u32[]{:S(2)}, u32[]{:S(2)}) collective-permute-start(f32[2,1,16,128]{3,2,1,0:T(8,128)S(1)} %slice.1368), channel_id=1, source_target_pairs={{0,2},{2,4},{4,6},{6,8},{8,10},{10,12},{12,14},{1,3},{3,5},{5,7},{... | collective-permute-start | bytes 49160 | tf_op jit(solution)/shard_map/ppermute | solution.py:14
  56.2 1.6 copy-start.74
  56.2 2.9 copy-start.72
  57.8 6.0 %collective-permute-start.8 = (f32[2,16,1,128]{3,2,1,0:T(1,128)S(1)}, f32[2,16,1,128]{3,2,1,0:T(1,128)S(1)}, u32[]{:S(2)}, u32[]{:S(2)}) collective-permute-start(f32[2,16,1,128]{3,2,1,0:T(1,128)S(1)} %copy-done.74), channel_id=1, source_target_pairs={{1,0},{3,2},{5,4},{7,6},{9,8},{11,10},{13,12},{15,14},{17,16},{19,... | collective-permute-start | bytes 49160 | tf_op jit(solution)/shard_map/ppermute | solution.py:14
  59.1 5.9 %collective-permute-start.9 = (f32[2,1,16,128]{3,2,1,0:T(8,128)S(1)}, f32[2,1,16,128]{3,2,1,0:T(8,128)S(1)}, u32[]{:S(2)}, u32[]{:S(2)}) collective-permute-start(f32[2,1,16,128]{3,2,1,0:T(8,128)S(1)} %copy-done.72), channel_id=1, source_target_pairs={{2,0},{4,2},{6,4},{8,6},{10,8},{12,10},{14,12},{3,1},{5,3},{7,5},{... | collective-permute-start | bytes 49160 | tf_op jit(solution)/shard_map/ppermute | solution.py:14
  66.9 1.2 copy-start.42
  67.0 1.2 copy-start.54
  67.0 1.2 copy-start.56
  68.3 9.8 %collective-permute-start.10 = (f32[2,16,1,128]{3,1,2,0:T(8,128)S(1)}, f32[2,16,1,128]{3,1,2,0:T(8,128)S(1)}, u32[]{:S(2)}, u32[]{:S(2)}) collective-permute-start(f32[2,16,1,128]{3,1,2,0:T(8,128)S(1)} %bitcast.594), channel_id=1, source_target_pairs={{0,1},{2,3},{4,5},{6,7},{8,9},{10,11},{12,13},{14,15},{16,17},{18,... | collective-permute-start | bytes 49160 | tf_op jit(solution)/shard_map/ppermute | solution.py:14
  74.5 4.5 %collective-permute-start.11 = (f32[2,1,16,128]{3,2,1,0:T(8,128)S(1)}, f32[2,1,16,128]{3,2,1,0:T(8,128)S(1)}, u32[]{:S(2)}, u32[]{:S(2)}) collective-permute-start(f32[2,1,16,128]{3,2,1,0:T(8,128)S(1)} %slice.1396), channel_id=1, source_target_pairs={{0,2},{2,4},{4,6},{6,8},{8,10},{10,12},{12,14},{1,3},{3,5},{5,7},{... | collective-permute-start | bytes 49160 | tf_op jit(solution)/shard_map/ppermute | solution.py:14
  84.6 3.0 copy-start.73
  86.1 2.7 copy-start.80
  86.1 6.4 %collective-permute-start.12 = (f32[2,16,1,128]{3,1,2,0:T(8,128)}, f32[2,16,1,128]{3,1,2,0:T(8,128)}, u32[]{:S(2)}, u32[]{:S(2)}) collective-permute-start(f32[2,16,1,128]{3,1,2,0:T(8,128)} %bitcast.197), channel_id=1, source_target_pairs={{1,0},{3,2},{5,4},{7,6},{9,8},{11,10},{13,12},{15,14},{17,16},{19,... | collective-permute-start | bytes 49160 | tf_op jit(solution)/shard_map/ppermute | solution.py:14
  87.5 5.7 %collective-permute-start.13 = (f32[2,1,16,128]{3,2,1,0:T(8,128)S(1)}, f32[2,1,16,128]{3,2,1,0:T(8,128)}, u32[]{:S(2)}, u32[]{:S(2)}) collective-permute-start(f32[2,1,16,128]{3,2,1,0:T(8,128)S(1)} %copy-done.73), channel_id=1, source_target_pairs={{2,0},{4,2},{6,4},{8,6},{10,8},{12,10},{14,12},{3,1},{5,3},{7,5},{... | collective-permute-start | bytes 49160 | tf_op jit(solution)/shard_map/ppermute | solution.py:14
  96.0 1.2 copy-start.57
  96.0 1.2 copy-start.61
  97.4 9.6 %collective-permute-start.14 = (f32[2,16,1,128]{3,1,2,0:T(8,128)S(1)}, f32[2,16,1,128]{3,1,2,0:T(8,128)S(1)}, u32[]{:S(2)}, u32[]{:S(2)}) collective-permute-start(f32[2,16,1,128]{3,1,2,0:T(8,128)S(1)} %bitcast.595), channel_id=1, source_target_pairs={{0,1},{2,3},{4,5},{6,7},{8,9},{10,11},{12,13},{14,15},{16,17},{18,... | collective-permute-start | bytes 49160 | tf_op jit(solution)/shard_map/ppermute | solution.py:14
  103.3 4.5 %collective-permute-start.15 = (f32[2,1,16,128]{3,2,1,0:T(8,128)S(1)}, f32[2,1,16,128]{3,2,1,0:T(8,128)S(1)}, u32[]{:S(2)}, u32[]{:S(2)}) collective-permute-start(f32[2,1,16,128]{3,2,1,0:T(8,128)S(1)} %slice.1424), channel_id=1, source_target_pairs={{0,2},{2,4},{4,6},{6,8},{8,10},{10,12},{12,14},{1,3},{3,5},{5,7},{... | collective-permute-start | bytes 49160 | tf_op jit(solution)/shard_map/ppermute | solution.py:14
  109.1 1.3 copy-start.81
  110.0 2.2 copy-start.62
  118.0 6.0 %collective-permute-start.16 = (f32[2,16,1,128]{3,1,2,0:T(8,128)S(1)}, f32[2,16,1,128]{3,1,2,0:T(8,128)S(1)}, u32[]{:S(2)}, u32[]{:S(2)}) collective-permute-start(f32[2,16,1,128]{3,1,2,0:T(8,128)S(1)} %bitcast.589), channel_id=1, source_target_pairs={{1,0},{3,2},{5,4},{7,6},{9,8},{11,10},{13,12},{15,14},{17,16},{19,... | collective-permute-start | bytes 49160 | tf_op jit(solution)/shard_map/ppermute | solution.py:14
  119.4 5.5 %collective-permute-start.17 = (f32[2,1,16,128]{3,2,1,0:T(8,128)S(1)}, f32[2,1,16,128]{3,2,1,0:T(8,128)S(1)}, u32[]{:S(2)}, u32[]{:S(2)}) collective-permute-start(f32[2,1,16,128]{3,2,1,0:T(8,128)S(1)} %slice.1440), channel_id=1, source_target_pairs={{2,0},{4,2},{6,4},{8,6},{10,8},{12,10},{14,12},{3,1},{5,3},{7,5},{... | collective-permute-start | bytes 49160 | tf_op jit(solution)/shard_map/ppermute | solution.py:14
  125.0 1.2 copy-start.4
  126.3 9.8 %collective-permute-start.18 = (f32[2,16,1,128]{3,1,2,0:T(8,128)S(1)}, f32[2,16,1,128]{3,1,2,0:T(8,128)S(1)}, u32[]{:S(2)}, u32[]{:S(2)}) collective-permute-start(f32[2,16,1,128]{3,1,2,0:T(8,128)S(1)} %bitcast.596), channel_id=1, source_target_pairs={{0,1},{2,3},{4,5},{6,7},{8,9},{10,11},{12,13},{14,15},{16,17},{18,... | collective-permute-start | bytes 49160 | tf_op jit(solution)/shard_map/ppermute | solution.py:14
  132.4 4.5 %collective-permute-start.19 = (f32[2,1,16,128]{3,2,1,0:T(8,128)S(1)}, f32[2,1,16,128]{3,2,1,0:T(8,128)S(1)}, u32[]{:S(2)}, u32[]{:S(2)}) collective-permute-start(f32[2,1,16,128]{3,2,1,0:T(8,128)S(1)} %slice.1453), channel_id=1, source_target_pairs={{0,2},{2,4},{4,6},{6,8},{8,10},{10,12},{12,14},{1,3},{3,5},{5,7},{... | collective-permute-start | bytes 49160 | tf_op jit(solution)/shard_map/ppermute | solution.py:14
  143.9 6.0 %collective-permute-start.20 = (f32[2,16,1,128]{3,1,2,0:T(8,128)S(1)}, f32[2,16,1,128]{3,1,2,0:T(8,128)S(1)}, u32[]{:S(2)}, u32[]{:S(2)}) collective-permute-start(f32[2,16,1,128]{3,1,2,0:T(8,128)S(1)} %bitcast.590), channel_id=1, source_target_pairs={{1,0},{3,2},{5,4},{7,6},{9,8},{11,10},{13,12},{15,14},{17,16},{19,... | collective-permute-start | bytes 49160 | tf_op jit(solution)/shard_map/ppermute | solution.py:14
  145.4 4.7 %collective-permute-start.21 = (f32[2,1,16,128]{3,2,1,0:T(8,128)S(1)}, f32[2,1,16,128]{3,2,1,0:T(8,128)S(1)}, u32[]{:S(2)}, u32[]{:S(2)}) collective-permute-start(f32[2,1,16,128]{3,2,1,0:T(8,128)S(1)} %slice.1473), channel_id=1, source_target_pairs={{2,0},{4,2},{6,4},{8,6},{10,8},{12,10},{14,12},{3,1},{5,3},{7,5},{... | collective-permute-start | bytes 49160 | tf_op jit(solution)/shard_map/ppermute | solution.py:14
  150.2 1.3 copy-start.5
  150.3 1.2 copy-start.12
  150.4 1.2 copy-start.26
  150.4 1.2 copy-start.29
  151.7 9.8 %collective-permute-start.22 = (f32[2,16,1,128]{3,1,2,0:T(8,128)S(1)}, f32[2,16,1,128]{3,1,2,0:T(8,128)S(1)}, u32[]{:S(2)}, u32[]{:S(2)}) collective-permute-start(f32[2,16,1,128]{3,1,2,0:T(8,128)S(1)} %bitcast.597), channel_id=1, source_target_pairs={{0,1},{2,3},{4,5},{6,7},{8,9},{10,11},{12,13},{14,15},{16,17},{18,... | collective-permute-start | bytes 49160 | tf_op jit(solution)/shard_map/ppermute | solution.py:14
  157.8 4.5 %collective-permute-start.23 = (f32[2,1,16,128]{3,2,1,0:T(8,128)S(1)}, f32[2,1,16,128]{3,2,1,0:T(8,128)S(1)}, u32[]{:S(2)}, u32[]{:S(2)}) collective-permute-start(f32[2,1,16,128]{3,2,1,0:T(8,128)S(1)} %slice.1486), channel_id=1, source_target_pairs={{0,2},{2,4},{4,6},{6,8},{8,10},{10,12},{12,14},{1,3},{3,5},{5,7},{... | collective-permute-start | bytes 49160 | tf_op jit(solution)/shard_map/ppermute | solution.py:14
  169.3 6.0 %collective-permute-start.24 = (f32[2,16,1,128]{3,1,2,0:T(8,128)S(1)}, f32[2,16,1,128]{3,1,2,0:T(8,128)S(1)}, u32[]{:S(2)}, u32[]{:S(2)}) collective-permute-start(f32[2,16,1,128]{3,1,2,0:T(8,128)S(1)} %bitcast.591), channel_id=1, source_target_pairs={{1,0},{3,2},{5,4},{7,6},{9,8},{11,10},{13,12},{15,14},{17,16},{19,... | collective-permute-start | bytes 49160 | tf_op jit(solution)/shard_map/ppermute | solution.py:14
  170.7 5.0 %collective-permute-start.25 = (f32[2,1,16,128]{3,2,1,0:T(8,128)S(1)}, f32[2,1,16,128]{3,2,1,0:T(8,128)S(1)}, u32[]{:S(2)}, u32[]{:S(2)}) collective-permute-start(f32[2,1,16,128]{3,2,1,0:T(8,128)S(1)} %slice.1504), channel_id=1, source_target_pairs={{2,0},{4,2},{6,4},{8,6},{10,8},{12,10},{14,12},{3,1},{5,3},{7,5},{... | collective-permute-start | bytes 49160 | tf_op jit(solution)/shard_map/ppermute | solution.py:14
  175.9 1.2 copy-start.6
  176.0 1.2 copy-start.13
  176.0 1.2 copy-start.27
  176.0 1.2 copy-start.30
  176.0 1.3 copy-start.39
  176.1 1.3 copy-start.50
  176.1 1.3 copy-start.52
  177.5 9.8 %collective-permute-start.26 = (f32[2,16,1,128]{3,1,2,0:T(8,128)S(1)}, f32[2,16,1,128]{3,1,2,0:T(8,128)S(1)}, u32[]{:S(2)}, u32[]{:S(2)}) collective-permute-start(f32[2,16,1,128]{3,1,2,0:T(8,128)S(1)} %bitcast.598), channel_id=1, source_target_pairs={{0,1},{2,3},{4,5},{6,7},{8,9},{10,11},{12,13},{14,15},{16,17},{18,... | collective-permute-start | bytes 49160 | tf_op jit(solution)/shard_map/ppermute | solution.py:14
  183.6 4.5 %collective-permute-start.27 = (f32[2,1,16,128]{3,2,1,0:T(8,128)S(1)}, f32[2,1,16,128]{3,2,1,0:T(8,128)S(1)}, u32[]{:S(2)}, u32[]{:S(2)}) collective-permute-start(f32[2,1,16,128]{3,2,1,0:T(8,128)S(1)} %slice.1517), channel_id=1, source_target_pairs={{0,2},{2,4},{4,6},{6,8},{8,10},{10,12},{12,14},{1,3},{3,5},{5,7},{... | collective-permute-start | bytes 49160 | tf_op jit(solution)/shard_map/ppermute | solution.py:14
  195.3 6.0 %collective-permute-start.28 = (f32[2,16,1,128]{3,2,1,0:T(1,128)S(1)}, f32[2,16,1,128]{3,2,1,0:T(1,128)S(1)}, u32[]{:S(2)}, u32[]{:S(2)}) collective-permute-start(f32[2,16,1,128]{3,2,1,0:T(1,128)S(1)} %slice.1285), channel_id=1, source_target_pairs={{1,0},{3,2},{5,4},{7,6},{9,8},{11,10},{13,12},{15,14},{17,16},{19,... | collective-permute-start | bytes 49160 | tf_op jit(solution)/shard_map/ppermute | solution.py:14
  196.7 4.7 %collective-permute-start.29 = (f32[2,1,16,128]{3,2,1,0:T(8,128)S(1)}, f32[2,1,16,128]{3,2,1,0:T(8,128)S(1)}, u32[]{:S(2)}, u32[]{:S(2)}) collective-permute-start(f32[2,1,16,128]{3,2,1,0:T(8,128)S(1)} %slice.1535), channel_id=1, source_target_pairs={{2,0},{4,2},{6,4},{8,6},{10,8},{12,10},{14,12},{3,1},{5,3},{7,5},{... | collective-permute-start | bytes 49160 | tf_op jit(solution)/shard_map/ppermute | solution.py:14
  201.5 1.2 copy-start.7
  201.7 1.2 copy-start.28
  201.7 1.2 copy-start.31
  201.7 1.2 copy-start.40
  201.7 1.3 copy-start.51
  203.1 9.8 %collective-permute-start.30 = (f32[2,16,1,128]{3,1,2,0:T(8,128)S(1)}, f32[2,16,1,128]{3,1,2,0:T(8,128)S(1)}, u32[]{:S(2)}, u32[]{:S(2)}) collective-permute-start(f32[2,16,1,128]{3,1,2,0:T(8,128)S(1)} %bitcast.599), channel_id=1, source_target_pairs={{0,1},{2,3},{4,5},{6,7},{8,9},{10,11},{12,13},{14,15},{16,17},{18,... | collective-permute-start | bytes 49160 | tf_op jit(solution)/shard_map/ppermute | solution.py:14
  209.3 4.5 %collective-permute-start.31 = (f32[2,1,16,128]{3,2,1,0:T(8,128)S(1)}, f32[2,1,16,128]{3,2,1,0:T(8,128)S(1)}, u32[]{:S(2)}, u32[]{:S(2)}) collective-permute-start(f32[2,1,16,128]{3,2,1,0:T(8,128)S(1)} %slice.1548), channel_id=1, source_target_pairs={{0,2},{2,4},{4,6},{6,8},{8,10},{10,12},{12,14},{1,3},{3,5},{5,7},{... | collective-permute-start | bytes 49160 | tf_op jit(solution)/shard_map/ppermute | solution.py:14
  (51 other events, 46.1 us)
Sparse Core Ops, SparseCore 0:
  217.1 75.4 reduce-scatter.1
where the time goes:
time: 329 us; the launch traced here: 327 us
  blocking collectives  100 us (30%)
  starting transfers between devices  99.3 us (30%)
  local copies, waits for them, and re-layouts  54.1 us (16%)
  waiting for transfers between devices  27.5 us (8%)
  between operations  19.4 us (6%)
  other arithmetic  18.6 us (6%)
  matrix products  7.47 us (2%)
    psum x1, blocking collectives, on_device(): misfit = lax.psum(local_misfit, ('tx', 'gx', 'gy'))  100 us
    ppermute x32, starting transfers between devices, shifted(): return lax.ppermute(x, axis, pairs)  99.2 us
    ppermute x32, waiting for transfers between devices, shifted(): return lax.ppermute(x, axis, pairs)  27.5 us
    unnamed x167, local copies, waits for them, and re-layouts  21.2 us
    scatter-add x4, local copies, waits for them, and re-layouts, on_device(): adj_e.at[0:2, :, :, ZREC]  14.4 us
    another operation x6, other arithmetic  10.1 us
  transfers between devices with their start and end apart: 33, of which 20 were waited for; matrix products, arithmetic and copies ran while one was open for 4% of the time, Pallas kernels for 0%

commit v1 on v0

--- a/solution.py
+++ b/solution.py
@@ -119,7 +119,7 @@
     local_misfit = jnp.float32(0.0)
     for step_idx in range(STEPS):
         local_misfit = local_misfit + 0.5 * jnp.sum(residuals[step_idx] * residuals[step_idx])
-    misfit = lax.psum(local_misfit, ("tx", "gx", "gy"))
+    misfit = lax.psum(lax.psum(local_misfit, ("gx", "gy")), "tx")
     tile_flag = footprint[0, 0, 0].astype(jnp.float32)
     gradient = jnp.stack([grad_h, grad_v]) * tile_flag
     groups_count = lax.axis_size("tx")

time: 329 us -> 316 us (0.960)
  blocking collectives: 100 us -> 84.4 us
    psum x1 -> x2, blocking collectives: 100 us -> 84.4 us  [on_device(): misfit = lax.psum(lax.psum(local_misfit, ('gx', 'gy')), 'tx')]
where the time goes in v1:
time: 316 us; the launch traced here: 314 us
  starting transfers between devices  99.1 us (31%)
  blocking collectives  84.4 us (27%)
  local copies, waits for them, and re-layouts  56 us (18%)
  waiting for transfers between devices  27.7 us (9%)
  other arithmetic  19.8 us (6%)
  between operations  19.3 us (6%)
  matrix products  7.44 us (2%)
    ppermute x32, starting transfers between devices, shifted(): return lax.ppermute(x, axis, pairs)  99.1 us
    psum x2, blocking collectives, on_device(): misfit = lax.psum(lax.psum(local_misfit, ('gx', 'gy')), 'tx')  84.4 us
    ppermute x32, waiting for transfers between devices, shifted(): return lax.ppermute(x, axis, pairs)  27.6 us
    unnamed x167, local copies, waits for them, and re-layouts  21.2 us
    scatter-add x4, local copies, waits for them, and re-layouts, on_device(): adj_e.at[0:2, :, :, ZREC]  16.3 us
    another operation x6, other arithmetic  11.3 us
  transfers between devices with their start and end apart: 33, of which 20 were waited for; matrix products, arithmetic and copies ran while one was open for 4% of the time, Pallas kernels for 0%

profile of v1, /device:TPU:1, one launch (start us, length us, event | category | flops | bytes accessed | tf_op | source)
XLA Modules:
  0.0 313.7 jit_solution(6891984223829156185)
XLA Ops:
  7.2 1.1 slice_bitcast_fusion
  8.3 1.3 collective-permute-start
  9.6 1.4 collective-permute-start.1
  15.4 1.9 and_reduce_fusion
  19.1 5.6 %collective-permute-start.2 = (f32[2,16,1,128]{3,1,2,0:T(8,128)S(1)}, f32[2,16,1,128]{3,1,2,0:T(8,128)S(1)}, u32[]{:S(2)}, u32[]{:S(2)}) collective-permute-start(f32[2,16,1,128]{3,1,2,0:T(8,128)S(1)} %bitcast.592), channel_id=1, source_target_pairs={{0,1},{2,3},{4,5},{6,7},{8,9},{10,11},{12,13},{14,15},{16,17},{18,... | collective-permute-start | bytes 49160 | tf_op jit(solution)/shard_map/ppermute | solution.py:14
  24.8 4.5 %collective-permute-start.3 = (f32[2,1,16,128]{3,2,1,0:T(8,128)S(1)}, f32[2,1,16,128]{3,2,1,0:T(8,128)S(1)}, u32[]{:S(2)}, u32[]{:S(2)}) collective-permute-start(f32[2,1,16,128]{3,2,1,0:T(8,128)S(1)} %slice.1340), channel_id=1, source_target_pairs={{0,2},{2,4},{4,6},{6,8},{8,10},{10,12},{12,14},{1,3},{3,5},{5,7},{... | collective-permute-start | bytes 49160 | tf_op jit(solution)/shard_map/ppermute | solution.py:14
  32.4 1.3 collective-permute-start.4
  33.7 1.3 collective-permute-start.5
  35.8 1.5 multiply_reduce_fusion.3
  37.5 0.9 reshape.515
  38.4 1.3 collective-permute-done.5
  41.6 6.1 %collective-permute-start.6 = (f32[2,16,1,128]{3,1,2,0:T(8,128)S(1)}, f32[2,16,1,128]{3,1,2,0:T(8,128)S(1)}, u32[]{:S(2)}, u32[]{:S(2)}) collective-permute-start(f32[2,16,1,128]{3,1,2,0:T(8,128)S(1)} %bitcast.593), channel_id=1, source_target_pairs={{0,1},{2,3},{4,5},{6,7},{8,9},{10,11},{12,13},{14,15},{16,17},{18,... | collective-permute-start | bytes 49160 | tf_op jit(solution)/shard_map/ppermute | solution.py:14
  47.7 3.7 %collective-permute-start.7 = (f32[2,1,16,128]{3,2,1,0:T(8,128)S(1)}, f32[2,1,16,128]{3,2,1,0:T(8,128)S(1)}, u32[]{:S(2)}, u32[]{:S(2)}) collective-permute-start(f32[2,1,16,128]{3,2,1,0:T(8,128)S(1)} %slice.1368), channel_id=1, source_target_pairs={{0,2},{2,4},{4,6},{6,8},{8,10},{10,12},{12,14},{1,3},{3,5},{5,7},{... | collective-permute-start | bytes 49160 | tf_op jit(solution)/shard_map/ppermute | solution.py:14
  56.2 1.6 multiply_reduce_fusion.2
  57.7 1.3 collective-permute-start.8
  59.0 1.3 collective-permute-start.9
  60.5 0.9 reshape.514
  61.4 2.3 collective-permute-done.8
  63.7 1.3 collective-permute-done.9
  65.0 0.9 slice_bitcast_fusion.79
  68.3 6.1 %collective-permute-start.10 = (f32[2,16,1,128]{3,1,2,0:T(8,128)S(1)}, f32[2,16,1,128]{3,1,2,0:T(8,128)S(1)}, u32[]{:S(2)}, u32[]{:S(2)}) collective-permute-start(f32[2,16,1,128]{3,1,2,0:T(8,128)S(1)} %bitcast.594), channel_id=1, source_target_pairs={{0,1},{2,3},{4,5},{6,7},{8,9},{10,11},{12,13},{14,15},{16,17},{18,... | collective-permute-start | bytes 49160 | tf_op jit(solution)/shard_map/ppermute | solution.py:14
  74.4 3.7 %collective-permute-start.11 = (f32[2,1,16,128]{3,2,1,0:T(8,128)S(1)}, f32[2,1,16,128]{3,2,1,0:T(8,128)S(1)}, u32[]{:S(2)}, u32[]{:S(2)}) collective-permute-start(f32[2,1,16,128]{3,2,1,0:T(8,128)S(1)} %slice.1396), channel_id=1, source_target_pairs={{0,2},{2,4},{4,6},{6,8},{8,10},{10,12},{12,14},{1,3},{3,5},{5,7},{... | collective-permute-start | bytes 49160 | tf_op jit(solution)/shard_map/ppermute | solution.py:14
  84.5 1.5 multiply_reduce_fusion.1
  86.1 1.4 collective-permute-start.12
  87.5 1.3 collective-permute-start.13
  89.6 1.6 reshape.513
  91.1 1.3 collective-permute-done.12
  93.9 1.0 slice_bitcast_fusion.77
  97.4 5.9 %collective-permute-start.14 = (f32[2,16,1,128]{3,1,2,0:T(8,128)S(1)}, f32[2,16,1,128]{3,1,2,0:T(8,128)S(1)}, u32[]{:S(2)}, u32[]{:S(2)}) collective-permute-start(f32[2,16,1,128]{3,1,2,0:T(8,128)S(1)} %bitcast.595), channel_id=1, source_target_pairs={{0,1},{2,3},{4,5},{6,7},{8,9},{10,11},{12,13},{14,15},{16,17},{18,... | collective-permute-start | bytes 49160 | tf_op jit(solution)/shard_map/ppermute | solution.py:14
  103.3 3.7 %collective-permute-start.15 = (f32[2,1,16,128]{3,2,1,0:T(8,128)S(1)}, f32[2,1,16,128]{3,2,1,0:T(8,128)S(1)}, u32[]{:S(2)}, u32[]{:S(2)}) collective-permute-start(f32[2,1,16,128]{3,2,1,0:T(8,128)S(1)} %slice.1424), channel_id=1, source_target_pairs={{0,2},{2,4},{4,6},{6,8},{8,10},{10,12},{12,14},{1,3},{3,5},{5,7},{... | collective-permute-start | bytes 49160 | tf_op jit(solution)/shard_map/ppermute | solution.py:14
  110.3 1.5 multiply_reduce_fusion
  112.2 2.0 add_select_fusion.3
  114.2 3.6 %scatter-add.14 = f32[3,16,16,128]{3,2,1,0:T(8,128)S(1)} dynamic-update-slice(f32[3,16,16,128]{3,2,1,0:T(8,128)S(1)} %get-tuple-element.51, f32[2,16,16,1]{3,2,1,0:T(8,128)S(1)} %add_select_fusion.3, s32[]{:T(128)} %bitcast.4, s32[]{:T(128)} %constant.106.clone.1, s32[]{:T(128)} %constant.106.clone.1, s32[]{:T(128)} %bitcast.5) | dynamic-update-slice | bytes 4100 | tf_op jit(solution)/shard_map/scatter-add | solution.py:112
  117.9 1.3 collective-permute-start.16
  119.3 1.3 collective-permute-start.17
  120.6 3.3 %collective-permute-done.16 = f32[2,16,1,128]{3,1,2,0:T(8,128)S(1)} collective-permute-done((f32[2,16,1,128]{3,1,2,0:T(8,128)S(1)}, f32[2,16,1,128]{3,1,2,0:T(8,128)S(1)}, u32[]{:S(2)}, u32[]{:S(2)}) %collective-permute-start.16) | collective-permute-done | bytes 16416 | tf_op jit(solution)/shard_map/ppermute | solution.py:14
  123.9 0.9 collective-permute-done.17
  126.2 6.1 %collective-permute-start.18 = (f32[2,16,1,128]{3,1,2,0:T(8,128)S(1)}, f32[2,16,1,128]{3,1,2,0:T(8,128)S(1)}, u32[]{:S(2)}, u32[]{:S(2)}) collective-permute-start(f32[2,16,1,128]{3,1,2,0:T(8,128)S(1)} %bitcast.596), channel_id=1, source_target_pairs={{0,1},{2,3},{4,5},{6,7},{8,9},{10,11},{12,13},{14,15},{16,17},{18,... | collective-permute-start | bytes 49160 | tf_op jit(solution)/shard_map/ppermute | solution.py:14
  132.3 3.7 %collective-permute-start.19 = (f32[2,1,16,128]{3,2,1,0:T(8,128)S(1)}, f32[2,1,16,128]{3,2,1,0:T(8,128)S(1)}, u32[]{:S(2)}, u32[]{:S(2)}) collective-permute-start(f32[2,1,16,128]{3,2,1,0:T(8,128)S(1)} %slice.1453), channel_id=1, source_target_pairs={{0,2},{2,4},{4,6},{6,8},{8,10},{10,12},{12,14},{1,3},{3,5},{5,7},{... | collective-permute-start | bytes 49160 | tf_op jit(solution)/shard_map/ppermute | solution.py:14
  137.2 0.9 copy-done.65
  138.2 2.0 add_select_fusion.2
  140.1 3.6 %scatter-add.15 = f32[3,16,16,128]{3,2,1,0:T(8,128)S(1)} dynamic-update-slice(f32[3,16,16,128]{3,2,1,0:T(8,128)S(1)} %copy.87, f32[2,16,16,1]{3,2,1,0:T(8,128)S(1)} %add_select_fusion.2, s32[]{:T(128)} %bitcast.4, s32[]{:T(128)} %constant.106.clone.1, s32[]{:T(128)} %constant.106.clone.1, s32[]{:T(128)} %bitcast.5) | dynamic-update-slice | bytes 4100 | tf_op jit(solution)/shard_map/scatter-add | solution.py:112
  143.8 1.3 collective-permute-start.20
  145.2 1.3 collective-permute-start.21
  146.5 3.3 %collective-permute-done.20 = f32[2,16,1,128]{3,1,2,0:T(8,128)S(1)} collective-permute-done((f32[2,16,1,128]{3,1,2,0:T(8,128)S(1)}, f32[2,16,1,128]{3,1,2,0:T(8,128)S(1)}, u32[]{:S(2)}, u32[]{:S(2)}) %collective-permute-start.20) | collective-permute-done | bytes 16416 | tf_op jit(solution)/shard_map/ppermute | solution.py:14
  151.5 6.1 %collective-permute-start.22 = (f32[2,16,1,128]{3,1,2,0:T(8,128)S(1)}, f32[2,16,1,128]{3,1,2,0:T(8,128)S(1)}, u32[]{:S(2)}, u32[]{:S(2)}) collective-permute-start(f32[2,16,1,128]{3,1,2,0:T(8,128)S(1)} %bitcast.597), channel_id=1, source_target_pairs={{0,1},{2,3},{4,5},{6,7},{8,9},{10,11},{12,13},{14,15},{16,17},{18,... | collective-permute-start | bytes 49160 | tf_op jit(solution)/shard_map/ppermute | solution.py:14
  157.7 3.7 %collective-permute-start.23 = (f32[2,1,16,128]{3,2,1,0:T(8,128)S(1)}, f32[2,1,16,128]{3,2,1,0:T(8,128)S(1)}, u32[]{:S(2)}, u32[]{:S(2)}) collective-permute-start(f32[2,1,16,128]{3,2,1,0:T(8,128)S(1)} %slice.1486), channel_id=1, source_target_pairs={{0,2},{2,4},{4,6},{6,8},{8,10},{10,12},{12,14},{1,3},{3,5},{5,7},{... | collective-permute-start | bytes 49160 | tf_op jit(solution)/shard_map/ppermute | solution.py:14
  162.6 0.9 copy-done.64
  163.5 2.7 add_select_fusion.1
  166.2 4.5 %scatter-add.16 = f32[3,16,16,128]{3,2,1,0:T(8,128)S(1)} dynamic-update-slice(f32[3,16,16,128]{3,2,1,0:T(8,128)S(1)} %copy.88, f32[2,16,16,1]{3,2,1,0:T(8,128)} %add_select_fusion.1, s32[]{:T(128)} %bitcast.4, s32[]{:T(128)} %constant.106.clone.1, s32[]{:T(128)} %constant.106.clone.1, s32[]{:T(128)} %bitcast.5) | dynamic-update-slice | bytes 4100 | tf_op jit(solution)/shard_map/scatter-add | solution.py:112
  170.8 1.3 collective-permute-start.24
  172.2 1.5 collective-permute-start.25
  173.7 3.1 collective-permute-done.24
  178.9 6.1 %collective-permute-start.26 = (f32[2,16,1,128]{3,1,2,0:T(8,128)S(1)}, f32[2,16,1,128]{3,1,2,0:T(8,128)S(1)}, u32[]{:S(2)}, u32[]{:S(2)}) collective-permute-start(f32[2,16,1,128]{3,1,2,0:T(8,128)S(1)} %bitcast.598), channel_id=1, source_target_pairs={{0,1},{2,3},{4,5},{6,7},{8,9},{10,11},{12,13},{14,15},{16,17},{18,... | collective-permute-start | bytes 49160 | tf_op jit(solution)/shard_map/ppermute | solution.py:14
  185.1 3.7 %collective-permute-start.27 = (f32[2,1,16,128]{3,2,1,0:T(8,128)S(1)}, f32[2,1,16,128]{3,2,1,0:T(8,128)S(1)}, u32[]{:S(2)}, u32[]{:S(2)}) collective-permute-start(f32[2,1,16,128]{3,2,1,0:T(8,128)S(1)} %slice.1517), channel_id=1, source_target_pairs={{0,2},{2,4},{4,6},{6,8},{8,10},{10,12},{12,14},{1,3},{3,5},{5,7},{... | collective-permute-start | bytes 49160 | tf_op jit(solution)/shard_map/ppermute | solution.py:14
  191.0 2.7 add_select_fusion
  193.7 4.5 %scatter-add.19 = f32[3,16,16,128]{3,2,1,0:T(8,128)S(1)} dynamic-update-slice(f32[3,16,16,128]{3,2,1,0:T(8,128)S(1)} %copy.89, f32[2,16,16,1]{3,2,1,0:T(8,128)} %add_select_fusion, s32[]{:T(128)} %bitcast.4, s32[]{:T(128)} %constant.106.clone.1, s32[]{:T(128)} %constant.106.clone.1, s32[]{:T(128)} %bitcast.5) | dynamic-update-slice | bytes 4100 | tf_op jit(solution)/shard_map/scatter-add | solution.py:112
  198.3 1.3 collective-permute-start.28
  199.7 1.3 collective-permute-start.29
  201.0 3.3 %collective-permute-done.28 = f32[2,16,1,128]{3,2,1,0:T(1,128)S(1)} collective-permute-done((f32[2,16,1,128]{3,2,1,0:T(1,128)S(1)}, f32[2,16,1,128]{3,2,1,0:T(1,128)S(1)}, u32[]{:S(2)}, u32[]{:S(2)}) %collective-permute-start.28) | collective-permute-done | bytes 16416 | tf_op jit(solution)/shard_map/ppermute | solution.py:14
  206.4 5.9 %collective-permute-start.30 = (f32[2,16,1,128]{3,1,2,0:T(8,128)S(1)}, f32[2,16,1,128]{3,1,2,0:T(8,128)S(1)}, u32[]{:S(2)}, u32[]{:S(2)}) collective-permute-start(f32[2,16,1,128]{3,1,2,0:T(8,128)S(1)} %bitcast.599), channel_id=1, source_target_pairs={{0,1},{2,3},{4,5},{6,7},{8,9},{10,11},{12,13},{14,15},{16,17},{18,... | collective-permute-start | bytes 49160 | tf_op jit(solution)/shard_map/ppermute | solution.py:14
  212.3 3.7 %collective-permute-start.31 = (f32[2,1,16,128]{3,2,1,0:T(8,128)S(1)}, f32[2,1,16,128]{3,2,1,0:T(8,128)S(1)}, u32[]{:S(2)}, u32[]{:S(2)}) collective-permute-start(f32[2,1,16,128]{3,2,1,0:T(8,128)S(1)} %slice.1548), channel_id=1, source_target_pairs={{0,2},{2,4},{4,6},{6,8},{8,10},{10,12},{12,14},{1,3},{3,5},{5,7},{... | collective-permute-start | bytes 49160 | tf_op jit(solution)/shard_map/ppermute | solution.py:14
  222.5 31.1 %psum.14 = f32[]{:T(128)} all-reduce(f32[]{:T(128)S(6)} %add.231), channel_id=1, replica_groups=mesh['tx'=16,'gx'=8,'gy'=2] {'gx','gy'}, use_global_device_ids=true, to_apply=%region_6.0 | all-reduce | flops 1 | bytes 8 | tf_op jit(solution)/shard_map/psum | solution.py:122
  253.5 53.3 %psum.15 = f32[]{:T(128)} all-reduce(f32[]{:T(128)} %psum.14), channel_id=1, replica_groups=mesh['tx'=16,'gx'=8,'gy'=2] {'tx'}, use_global_device_ids=true, to_apply=%region_7.0 | all-reduce | flops 1 | bytes 8 | tf_op jit(solution)/shard_map/psum | solution.py:122
  (398 shorter events, 49.0 us)
Async XLA Ops:
  7.2 3.9 %copy-start = (f32[1,6,16,16,128]{4,3,2,1,0:T(8,128)S(1)}, f32[1,6,16,16,128]{4,3,2,1,0:T(8,128)}, u32[]{:S(2)}) copy-start(f32[1,6,16,16,128]{4,3,2,1,0:T(8,128)} %param.18) | copy-start | bytes 2359300
  7.2 299.7 %reduce-scatter.2.cloned.1.call-start = ((), (), s32[]{:S(2)}) async-start(), calls=%async_computation.1 | async-start | bytes 278528 | tf_op jit(solution)/shard_map/reduce_scatter | solution.py:129
  8.3 10.5 %collective-permute-start = (f32[2,16,1,128]{3,2,1,0:T(1,128)S(1)}, f32[2,16,1,128]{3,2,1,0:T(1,128)S(1)}, u32[]{:S(2)}, u32[]{:S(2)}) collective-permute-start(f32[2,16,1,128]{3,2,1,0:T(1,128)S(1)} %slice.1044), channel_id=1, source_target_pairs={{1,0},{3,2},{5,4},{7,6},{9,8},{11,10},{13,12},{15,14},{17,16},{19,... | collective-permute-start | bytes 49160 | tf_op jit(solution)/shard_map/ppermute | solution.py:14
  9.6 4.3 %copy-start.3 = (f32[1,6,16,16,128]{4,3,2,1,0:T(8,128)S(1)}, f32[1,6,16,16,128]{4,3,2,1,0:T(8,128)}, u32[]{:S(2)}) copy-start(f32[1,6,16,16,128]{4,3,2,1,0:T(8,128)} %param.19) | copy-start | bytes 2359300
  9.6 9.2 %collective-permute-start.1 = (f32[2,1,16,128]{3,2,1,0:T(8,128)S(1)}, f32[2,1,16,128]{3,2,1,0:T(8,128)S(1)}, u32[]{:S(2)}, u32[]{:S(2)}) collective-permute-start(f32[2,1,16,128]{3,2,1,0:T(8,128)S(1)} %slice.1328), channel_id=1, source_target_pairs={{2,0},{4,2},{6,4},{8,6},{10,8},{12,10},{14,12},{3,1},{5,3},{7,5},{... | collective-permute-start | bytes 49160 | tf_op jit(solution)/shard_map/ppermute | solution.py:14
  18.9 21.9 %copy-start.8 = (f32[1,16,16,128]{3,2,1,0:T(8,128)}, f32[1,16,16,128]{3,2,1,0:T(8,128)S(1)}, u32[]{:S(2)}) copy-start(f32[1,16,16,128]{3,2,1,0:T(8,128)S(1)} %fusion.33) | copy-start | bytes 393220
  19.1 10.2 %collective-permute-start.2 = (f32[2,16,1,128]{3,1,2,0:T(8,128)S(1)}, f32[2,16,1,128]{3,1,2,0:T(8,128)S(1)}, u32[]{:S(2)}, u32[]{:S(2)}) collective-permute-start(f32[2,16,1,128]{3,1,2,0:T(8,128)S(1)} %bitcast.592), channel_id=1, source_target_pairs={{0,1},{2,3},{4,5},{6,7},{8,9},{10,11},{12,13},{14,15},{16,17},{18,... | collective-permute-start | bytes 49160 | tf_op jit(solution)/shard_map/ppermute | solution.py:14
  24.8 5.4 %collective-permute-start.3 = (f32[2,1,16,128]{3,2,1,0:T(8,128)S(1)}, f32[2,1,16,128]{3,2,1,0:T(8,128)S(1)}, u32[]{:S(2)}, u32[]{:S(2)}) collective-permute-start(f32[2,1,16,128]{3,2,1,0:T(8,128)S(1)} %slice.1340), channel_id=1, source_target_pairs={{0,2},{2,4},{4,6},{6,8},{8,10},{10,12},{12,14},{1,3},{3,5},{5,7},{... | collective-permute-start | bytes 49160 | tf_op jit(solution)/shard_map/ppermute | solution.py:14
  32.4 6.0 %collective-permute-start.4 = (f32[2,16,1,128]{3,2,1,0:T(1,128)S(1)}, f32[2,16,1,128]{3,2,1,0:T(1,128)S(1)}, u32[]{:S(2)}, u32[]{:S(2)}) collective-permute-start(f32[2,16,1,128]{3,2,1,0:T(1,128)S(1)} %slice.1076), channel_id=1, source_target_pairs={{1,0},{3,2},{5,4},{7,6},{9,8},{11,10},{13,12},{15,14},{17,16},{19,... | collective-permute-start | bytes 49160 | tf_op jit(solution)/shard_map/ppermute | solution.py:14
  33.7 6.0 %collective-permute-start.5 = (f32[2,1,16,128]{3,2,1,0:T(8,128)S(1)}, f32[2,1,16,128]{3,2,1,0:T(8,128)S(1)}, u32[]{:S(2)}, u32[]{:S(2)}) collective-permute-start(f32[2,1,16,128]{3,2,1,0:T(8,128)S(1)} %slice.1355), channel_id=1, source_target_pairs={{2,0},{4,2},{6,4},{8,6},{10,8},{12,10},{14,12},{3,1},{5,3},{7,5},{... | collective-permute-start | bytes 49160 | tf_op jit(solution)/shard_map/ppermute | solution.py:14
  41.6 9.8 %collective-permute-start.6 = (f32[2,16,1,128]{3,1,2,0:T(8,128)S(1)}, f32[2,16,1,128]{3,1,2,0:T(8,128)S(1)}, u32[]{:S(2)}, u32[]{:S(2)}) collective-permute-start(f32[2,16,1,128]{3,1,2,0:T(8,128)S(1)} %bitcast.593), channel_id=1, source_target_pairs={{0,1},{2,3},{4,5},{6,7},{8,9},{10,11},{12,13},{14,15},{16,17},{18,... | collective-permute-start | bytes 49160 | tf_op jit(solution)/shard_map/ppermute | solution.py:14
  47.7 4.5 %collective-permute-start.7 = (f32[2,1,16,128]{3,2,1,0:T(8,128)S(1)}, f32[2,1,16,128]{3,2,1,0:T(8,128)S(1)}, u32[]{:S(2)}, u32[]{:S(2)}) collective-permute-start(f32[2,1,16,128]{3,2,1,0:T(8,128)S(1)} %slice.1368), channel_id=1, source_target_pairs={{0,2},{2,4},{4,6},{6,8},{8,10},{10,12},{12,14},{1,3},{3,5},{5,7},{... | collective-permute-start | bytes 49160 | tf_op jit(solution)/shard_map/ppermute | solution.py:14
  56.2 1.6 copy-start.74
  56.2 2.9 copy-start.72
  57.7 6.0 %collective-permute-start.8 = (f32[2,16,1,128]{3,2,1,0:T(1,128)S(1)}, f32[2,16,1,128]{3,2,1,0:T(1,128)S(1)}, u32[]{:S(2)}, u32[]{:S(2)}) collective-permute-start(f32[2,16,1,128]{3,2,1,0:T(1,128)S(1)} %copy-done.74), channel_id=1, source_target_pairs={{1,0},{3,2},{5,4},{7,6},{9,8},{11,10},{13,12},{15,14},{17,16},{19,... | collective-permute-start | bytes 49160 | tf_op jit(solution)/shard_map/ppermute | solution.py:14
  59.0 5.9 %collective-permute-start.9 = (f32[2,1,16,128]{3,2,1,0:T(8,128)S(1)}, f32[2,1,16,128]{3,2,1,0:T(8,128)S(1)}, u32[]{:S(2)}, u32[]{:S(2)}) collective-permute-start(f32[2,1,16,128]{3,2,1,0:T(8,128)S(1)} %copy-done.72), channel_id=1, source_target_pairs={{2,0},{4,2},{6,4},{8,6},{10,8},{12,10},{14,12},{3,1},{5,3},{7,5},{... | collective-permute-start | bytes 49160 | tf_op jit(solution)/shard_map/ppermute | solution.py:14
  66.9 1.2 copy-start.42
  67.0 1.2 copy-start.54
  67.0 1.2 copy-start.56
  68.3 9.8 %collective-permute-start.10 = (f32[2,16,1,128]{3,1,2,0:T(8,128)S(1)}, f32[2,16,1,128]{3,1,2,0:T(8,128)S(1)}, u32[]{:S(2)}, u32[]{:S(2)}) collective-permute-start(f32[2,16,1,128]{3,1,2,0:T(8,128)S(1)} %bitcast.594), channel_id=1, source_target_pairs={{0,1},{2,3},{4,5},{6,7},{8,9},{10,11},{12,13},{14,15},{16,17},{18,... | collective-permute-start | bytes 49160 | tf_op jit(solution)/shard_map/ppermute | solution.py:14
  74.4 4.5 %collective-permute-start.11 = (f32[2,1,16,128]{3,2,1,0:T(8,128)S(1)}, f32[2,1,16,128]{3,2,1,0:T(8,128)S(1)}, u32[]{:S(2)}, u32[]{:S(2)}) collective-permute-start(f32[2,1,16,128]{3,2,1,0:T(8,128)S(1)} %slice.1396), channel_id=1, source_target_pairs={{0,2},{2,4},{4,6},{6,8},{8,10},{10,12},{12,14},{1,3},{3,5},{5,7},{... | collective-permute-start | bytes 49160 | tf_op jit(solution)/shard_map/ppermute | solution.py:14
  84.5 2.9 copy-start.73
  86.1 2.7 copy-start.80
  86.1 6.4 %collective-permute-start.12 = (f32[2,16,1,128]{3,1,2,0:T(8,128)}, f32[2,16,1,128]{3,1,2,0:T(8,128)}, u32[]{:S(2)}, u32[]{:S(2)}) collective-permute-start(f32[2,16,1,128]{3,1,2,0:T(8,128)} %bitcast.197), channel_id=1, source_target_pairs={{1,0},{3,2},{5,4},{7,6},{9,8},{11,10},{13,12},{15,14},{17,16},{19,... | collective-permute-start | bytes 49160 | tf_op jit(solution)/shard_map/ppermute | solution.py:14
  87.5 5.7 %collective-permute-start.13 = (f32[2,1,16,128]{3,2,1,0:T(8,128)S(1)}, f32[2,1,16,128]{3,2,1,0:T(8,128)}, u32[]{:S(2)}, u32[]{:S(2)}) collective-permute-start(f32[2,1,16,128]{3,2,1,0:T(8,128)S(1)} %copy-done.73), channel_id=1, source_target_pairs={{2,0},{4,2},{6,4},{8,6},{10,8},{12,10},{14,12},{3,1},{5,3},{7,5},{... | collective-permute-start | bytes 49160 | tf_op jit(solution)/shard_map/ppermute | solution.py:14
  96.0 1.2 copy-start.57
  96.0 1.2 copy-start.61
  97.4 9.6 %collective-permute-start.14 = (f32[2,16,1,128]{3,1,2,0:T(8,128)S(1)}, f32[2,16,1,128]{3,1,2,0:T(8,128)S(1)}, u32[]{:S(2)}, u32[]{:S(2)}) collective-permute-start(f32[2,16,1,128]{3,1,2,0:T(8,128)S(1)} %bitcast.595), channel_id=1, source_target_pairs={{0,1},{2,3},{4,5},{6,7},{8,9},{10,11},{12,13},{14,15},{16,17},{18,... | collective-permute-start | bytes 49160 | tf_op jit(solution)/shard_map/ppermute | solution.py:14
  103.3 4.5 %collective-permute-start.15 = (f32[2,1,16,128]{3,2,1,0:T(8,128)S(1)}, f32[2,1,16,128]{3,2,1,0:T(8,128)S(1)}, u32[]{:S(2)}, u32[]{:S(2)}) collective-permute-start(f32[2,1,16,128]{3,2,1,0:T(8,128)S(1)} %slice.1424), channel_id=1, source_target_pairs={{0,2},{2,4},{4,6},{6,8},{8,10},{10,12},{12,14},{1,3},{3,5},{5,7},{... | collective-permute-start | bytes 49160 | tf_op jit(solution)/shard_map/ppermute | solution.py:14
  109.1 1.3 copy-start.81
  110.0 2.2 copy-start.62
  117.9 6.0 %collective-permute-start.16 = (f32[2,16,1,128]{3,1,2,0:T(8,128)S(1)}, f32[2,16,1,128]{3,1,2,0:T(8,128)S(1)}, u32[]{:S(2)}, u32[]{:S(2)}) collective-permute-start(f32[2,16,1,128]{3,1,2,0:T(8,128)S(1)} %bitcast.589), channel_id=1, source_target_pairs={{1,0},{3,2},{5,4},{7,6},{9,8},{11,10},{13,12},{15,14},{17,16},{19,... | collective-permute-start | bytes 49160 | tf_op jit(solution)/shard_map/ppermute | solution.py:14
  119.3 5.5 %collective-permute-start.17 = (f32[2,1,16,128]{3,2,1,0:T(8,128)S(1)}, f32[2,1,16,128]{3,2,1,0:T(8,128)S(1)}, u32[]{:S(2)}, u32[]{:S(2)}) collective-permute-start(f32[2,1,16,128]{3,2,1,0:T(8,128)S(1)} %slice.1440), channel_id=1, source_target_pairs={{2,0},{4,2},{6,4},{8,6},{10,8},{12,10},{14,12},{3,1},{5,3},{7,5},{... | collective-permute-start | bytes 49160 | tf_op jit(solution)/shard_map/ppermute | solution.py:14
  124.9 1.2 copy-start.4
  126.2 9.8 %collective-permute-start.18 = (f32[2,16,1,128]{3,1,2,0:T(8,128)S(1)}, f32[2,16,1,128]{3,1,2,0:T(8,128)S(1)}, u32[]{:S(2)}, u32[]{:S(2)}) collective-permute-start(f32[2,16,1,128]{3,1,2,0:T(8,128)S(1)} %bitcast.596), channel_id=1, source_target_pairs={{0,1},{2,3},{4,5},{6,7},{8,9},{10,11},{12,13},{14,15},{16,17},{18,... | collective-permute-start | bytes 49160 | tf_op jit(solution)/shard_map/ppermute | solution.py:14
  132.3 4.5 %collective-permute-start.19 = (f32[2,1,16,128]{3,2,1,0:T(8,128)S(1)}, f32[2,1,16,128]{3,2,1,0:T(8,128)S(1)}, u32[]{:S(2)}, u32[]{:S(2)}) collective-permute-start(f32[2,1,16,128]{3,2,1,0:T(8,128)S(1)} %slice.1453), channel_id=1, source_target_pairs={{0,2},{2,4},{4,6},{6,8},{8,10},{10,12},{12,14},{1,3},{3,5},{5,7},{... | collective-permute-start | bytes 49160 | tf_op jit(solution)/shard_map/ppermute | solution.py:14
  143.8 6.0 %collective-permute-start.20 = (f32[2,16,1,128]{3,1,2,0:T(8,128)S(1)}, f32[2,16,1,128]{3,1,2,0:T(8,128)S(1)}, u32[]{:S(2)}, u32[]{:S(2)}) collective-permute-start(f32[2,16,1,128]{3,1,2,0:T(8,128)S(1)} %bitcast.590), channel_id=1, source_target_pairs={{1,0},{3,2},{5,4},{7,6},{9,8},{11,10},{13,12},{15,14},{17,16},{19,... | collective-permute-start | bytes 49160 | tf_op jit(solution)/shard_map/ppermute | solution.py:14
  145.2 4.7 %collective-permute-start.21 = (f32[2,1,16,128]{3,2,1,0:T(8,128)S(1)}, f32[2,1,16,128]{3,2,1,0:T(8,128)S(1)}, u32[]{:S(2)}, u32[]{:S(2)}) collective-permute-start(f32[2,1,16,128]{3,2,1,0:T(8,128)S(1)} %slice.1473), channel_id=1, source_target_pairs={{2,0},{4,2},{6,4},{8,6},{10,8},{12,10},{14,12},{3,1},{5,3},{7,5},{... | collective-permute-start | bytes 49160 | tf_op jit(solution)/shard_map/ppermute | solution.py:14
  150.1 1.3 copy-start.5
  150.2 1.2 copy-start.12
  150.3 1.2 copy-start.26
  150.3 1.2 copy-start.29
  151.5 9.8 %collective-permute-start.22 = (f32[2,16,1,128]{3,1,2,0:T(8,128)S(1)}, f32[2,16,1,128]{3,1,2,0:T(8,128)S(1)}, u32[]{:S(2)}, u32[]{:S(2)}) collective-permute-start(f32[2,16,1,128]{3,1,2,0:T(8,128)S(1)} %bitcast.597), channel_id=1, source_target_pairs={{0,1},{2,3},{4,5},{6,7},{8,9},{10,11},{12,13},{14,15},{16,17},{18,... | collective-permute-start | bytes 49160 | tf_op jit(solution)/shard_map/ppermute | solution.py:14
  157.7 4.5 %collective-permute-start.23 = (f32[2,1,16,128]{3,2,1,0:T(8,128)S(1)}, f32[2,1,16,128]{3,2,1,0:T(8,128)S(1)}, u32[]{:S(2)}, u32[]{:S(2)}) collective-permute-start(f32[2,1,16,128]{3,2,1,0:T(8,128)S(1)} %slice.1486), channel_id=1, source_target_pairs={{0,2},{2,4},{4,6},{6,8},{8,10},{10,12},{12,14},{1,3},{3,5},{5,7},{... | collective-permute-start | bytes 49160 | tf_op jit(solution)/shard_map/ppermute | solution.py:14
  170.8 6.0 %collective-permute-start.24 = (f32[2,16,1,128]{3,1,2,0:T(8,128)S(1)}, f32[2,16,1,128]{3,1,2,0:T(8,128)S(1)}, u32[]{:S(2)}, u32[]{:S(2)}) collective-permute-start(f32[2,16,1,128]{3,1,2,0:T(8,128)S(1)} %bitcast.591), channel_id=1, source_target_pairs={{1,0},{3,2},{5,4},{7,6},{9,8},{11,10},{13,12},{15,14},{17,16},{19,... | collective-permute-start | bytes 49160 | tf_op jit(solution)/shard_map/ppermute | solution.py:14
  172.2 5.0 %collective-permute-start.25 = (f32[2,1,16,128]{3,2,1,0:T(8,128)S(1)}, f32[2,1,16,128]{3,2,1,0:T(8,128)S(1)}, u32[]{:S(2)}, u32[]{:S(2)}) collective-permute-start(f32[2,1,16,128]{3,2,1,0:T(8,128)S(1)} %slice.1504), channel_id=1, source_target_pairs={{2,0},{4,2},{6,4},{8,6},{10,8},{12,10},{14,12},{3,1},{5,3},{7,5},{... | collective-permute-start | bytes 49160 | tf_op jit(solution)/shard_map/ppermute | solution.py:14
  177.3 1.2 copy-start.6
  177.4 1.2 copy-start.13
  177.4 1.2 copy-start.27
  177.5 1.2 copy-start.30
  177.5 1.3 copy-start.39
  177.6 1.3 copy-start.50
  177.6 1.3 copy-start.52
  178.9 9.8 %collective-permute-start.26 = (f32[2,16,1,128]{3,1,2,0:T(8,128)S(1)}, f32[2,16,1,128]{3,1,2,0:T(8,128)S(1)}, u32[]{:S(2)}, u32[]{:S(2)}) collective-permute-start(f32[2,16,1,128]{3,1,2,0:T(8,128)S(1)} %bitcast.598), channel_id=1, source_target_pairs={{0,1},{2,3},{4,5},{6,7},{8,9},{10,11},{12,13},{14,15},{16,17},{18,... | collective-permute-start | bytes 49160 | tf_op jit(solution)/shard_map/ppermute | solution.py:14
  185.1 4.5 %collective-permute-start.27 = (f32[2,1,16,128]{3,2,1,0:T(8,128)S(1)}, f32[2,1,16,128]{3,2,1,0:T(8,128)S(1)}, u32[]{:S(2)}, u32[]{:S(2)}) collective-permute-start(f32[2,1,16,128]{3,2,1,0:T(8,128)S(1)} %slice.1517), channel_id=1, source_target_pairs={{0,2},{2,4},{4,6},{6,8},{8,10},{10,12},{12,14},{1,3},{3,5},{5,7},{... | collective-permute-start | bytes 49160 | tf_op jit(solution)/shard_map/ppermute | solution.py:14
  198.3 6.0 %collective-permute-start.28 = (f32[2,16,1,128]{3,2,1,0:T(1,128)S(1)}, f32[2,16,1,128]{3,2,1,0:T(1,128)S(1)}, u32[]{:S(2)}, u32[]{:S(2)}) collective-permute-start(f32[2,16,1,128]{3,2,1,0:T(1,128)S(1)} %slice.1285), channel_id=1, source_target_pairs={{1,0},{3,2},{5,4},{7,6},{9,8},{11,10},{13,12},{15,14},{17,16},{19,... | collective-permute-start | bytes 49160 | tf_op jit(solution)/shard_map/ppermute | solution.py:14
  199.7 4.9 %collective-permute-start.29 = (f32[2,1,16,128]{3,2,1,0:T(8,128)S(1)}, f32[2,1,16,128]{3,2,1,0:T(8,128)S(1)}, u32[]{:S(2)}, u32[]{:S(2)}) collective-permute-start(f32[2,1,16,128]{3,2,1,0:T(8,128)S(1)} %slice.1535), channel_id=1, source_target_pairs={{2,0},{4,2},{6,4},{8,6},{10,8},{12,10},{14,12},{3,1},{5,3},{7,5},{... | collective-permute-start | bytes 49160 | tf_op jit(solution)/shard_map/ppermute | solution.py:14
  204.7 1.2 copy-start.7
  204.9 1.2 copy-start.28
  204.9 1.2 copy-start.31
  204.9 1.2 copy-start.40
  204.9 1.3 copy-start.51
  206.4 9.6 %collective-permute-start.30 = (f32[2,16,1,128]{3,1,2,0:T(8,128)S(1)}, f32[2,16,1,128]{3,1,2,0:T(8,128)S(1)}, u32[]{:S(2)}, u32[]{:S(2)}) collective-permute-start(f32[2,16,1,128]{3,1,2,0:T(8,128)S(1)} %bitcast.599), channel_id=1, source_target_pairs={{0,1},{2,3},{4,5},{6,7},{8,9},{10,11},{12,13},{14,15},{16,17},{18,... | collective-permute-start | bytes 49160 | tf_op jit(solution)/shard_map/ppermute | solution.py:14
  212.3 4.5 %collective-permute-start.31 = (f32[2,1,16,128]{3,2,1,0:T(8,128)S(1)}, f32[2,1,16,128]{3,2,1,0:T(8,128)S(1)}, u32[]{:S(2)}, u32[]{:S(2)}) collective-permute-start(f32[2,1,16,128]{3,2,1,0:T(8,128)S(1)} %slice.1548), channel_id=1, source_target_pairs={{0,2},{2,4},{4,6},{6,8},{8,10},{10,12},{12,14},{1,3},{3,5},{5,7},{... | collective-permute-start | bytes 49160 | tf_op jit(solution)/shard_map/ppermute | solution.py:14
  (51 other events, 46.2 us)
Sparse Core Ops, SparseCore 0:
  220.1 75.7 reduce-scatter.1
